TPU v7x, 256 devices: a whole 4x4x8 slice. The times are simulated.
256 devices in a mesh: rep: 16 (over y, x), fsdp: 16 (over z, core).
Axes of the slice: x: 4, y: 4, z: 8, core: 2. Of those that a mesh axis runs over, the one named last changes fastest.
Arguments:
- hidden_acts: bfloat16 [16, 8192, 512], P('rep', 'fsdp'), may hold values from -6 to 6
- out_grads: bfloat16 [16, 8192, 8192], P('rep', 'fsdp'), may hold values from -0.15625 to 0.15625
- anchor: float32 [512, 8192], P('fsdp'), may hold values from -6 to 6
- drift: float32 [16, 512, 8192], P('rep', 'fsdp'), may hold values from -120 to 120, as said below
- adam_first: float32 [16, 512, 8192], P('rep', 'fsdp'), may hold values from -6 to 6
- adam_second: float32 [16, 512, 8192], P('rep', 'fsdp'), may hold values from 0.3 to 3
- outer_momentum: float32 [512, 8192], P('fsdp'), may hold values from -6 to 6
Outputs:
- new_first: float32 [16, 512, 8192], P('rep', 'fsdp')
- new_second: float32 [16, 512, 8192], P('rep', 'fsdp')
- new_momentum: float32 [512, 8192], P('fsdp')
- new_anchor: float32 [512, 8192], P('fsdp')
Inputs may be any that keep to these rules, and one draw needn't show every extreme that they name: drift entries are finite reals.
All inputs are finite; a program needn't handle non-finite values.
Results may differ from a plain program's by a relative error of at most 0.0003.
Values sent between devices are 32-bit elements; how exact they have to be, the bound alone decides.
No kernel may reach another device: no remote copies, remote signals or barrier semaphores. Data moves between devices by JAX's collectives and lax.ppermute only.
A program may use at most 128 MiB of HBM per device.

v0:
```python
import math
import jax
import jax.numpy as jnp
from jax import lax
from jax.sharding import PartitionSpec as P

D = 8192
INNER_STEP = 100
beta_first = 0.9
beta_second = 0.95
inner_rate = 0.5
decay_weight = 0.1
outer_rate = 0.7
momentum_coef = 0.9


def outer_update(average, squares, ceiling, momentum_old, anchor_old):
    factor = ceiling / jnp.maximum(jnp.sqrt(squares), ceiling)
    momentum = momentum_coef * momentum_old + factor * average
    updated = anchor_old - outer_rate * (factor * average + momentum_coef * momentum)
    return (momentum, updated)


def per_device(hidden_acts, out_grads, anchor, drift, adam_first, adam_second, outer_momentum):
    activations = hidden_acts[0]
    cotangent = out_grads[0]
    rows_dev = anchor.shape[0]
    gradient = lax.psum_scatter(
        lax.dot_general(
            activations, cotangent, (((0,), (0,)), ((), ())), preferred_element_type=jnp.float32
        ),
        "fsdp",
        scatter_dimension=0,
        tiled=True,
    )
    correction_one = 1.0 - beta_first**INNER_STEP
    correction_two = 1.0 - beta_second**INNER_STEP
    own_drift = drift[0]
    moment_one = beta_first * adam_first[0] + (1.0 - beta_first) * gradient
    moment_two = beta_second * adam_second[0] + (1.0 - beta_second) * gradient * gradient
    update = moment_one / correction_one / (
        jnp.sqrt(moment_two / correction_two) + 1e-08
    ) + decay_weight * (anchor + own_drift)
    pseudo = inner_rate * update - own_drift
    replicas = lax.axis_size("rep")
    ceiling = 0.3 * math.sqrt(rows_dev * lax.axis_size("fsdp") * D)
    average = lax.psum(pseudo, "rep") / replicas
    squares = lax.psum(jnp.sum(average * average), "fsdp")
    momentum, updated = outer_update(average, squares, ceiling, outer_momentum, anchor)
    return (moment_one[None], moment_two[None], momentum, updated)


def solution(mesh):
    return jax.shard_map(
        per_device,
        mesh=mesh,
        in_specs=(
            P("rep", "fsdp", None),
            P("rep", "fsdp", None),
            P("fsdp", None),
            P("rep", "fsdp", None),
            P("rep", "fsdp", None),
            P("rep", "fsdp", None),
            P("fsdp", None),
        ),
        out_specs=(
            P("rep", "fsdp", None),
            P("rep", "fsdp", None),
            P("fsdp", None),
            P("fsdp", None),
        ),
        check_vma=False,
    )
```

profile of v0, /device:TPU:1, one launch (start us, length us, event | category | flops | bytes accessed | tf_op | source)
XLA Modules:
  0.0 261.7 jit_solution(1608500180151418882)
XLA Ops:
  7.2 0.0 copy-start
  7.2 0.0 reduce-scatter.2.cloned.1.call-start
  7.2 1.0 copy-done
  8.2 11.5 %fusion = f32[512,8192]{1,0:T(8,128)} fusion(bf16[1,512,8192]{2,1,0:T(8,128)(2,1)} %param.8, bf16[1,512,512]{2,1,0:T(8,128)(2,1)S(1)} %copy-done), kind=kOutput, calls=%fused_computation | convolution fusion | flops 4294967296 | bytes 25690112 | tf_op jit(solution)/shard_map/dot_general | solution.py:29
  19.7 0.0 copy-start.1
  19.7 0.0 reduce-scatter.2.cloned.1.call-update
  19.7 0.0 copy-start.2
  19.7 0.0 all-reduce.2.cloned.1.call-start
  19.8 103.3 %reduce-scatter.2.cloned.1.call-done = f32[32,8192]{1,0:T(8,128)} async-done(((f32[512,8192]{1,0:T(8,128)}), f32[32,8192]{1,0:T(8,128)}) %reduce-scatter.2.cloned.1.call-update) | async-done | bytes 1048592 | tf_op jit(solution)/shard_map/reduce_scatter | solution.py:28
  123.1 0.0 copy-done.1
  123.1 4.3 %bitcast_subtract_fusion = (f32[32,8192]{1,0:T(8,128)}, f32[1,32,8192]{2,1,0:T(8,128)}, f32[1,32,8192]{2,1,0:T(8,128)}) fusion(f32[1,32,8192]{2,1,0:T(8,128)} %param.10, f32[32,8192]{1,0:T(8,128)S(1)} %copy-done.1, f32[32,8192]{1,0:T(8,128)} %reduce-scatter.2.cloned.1.call-done, f32[1,32,8192]{2,1,0:T(8,128)} %param.11, f32[1,32,8192]{2,1,0:T(8,128)} %param.12), kind=kLoop, calls=%fused_computation.4 | loop fusion | flops 4194304 | bytes 8388608 | tf_op jit(solution)/shard_map/sub | solution.py:44
  127.5 0.0 all-reduce.2.cloned.1.call-update
  127.5 95.5 %all-reduce.2.cloned.1.call-done = f32[32,8192]{1,0:T(8,128)} async-done(((f32[32,8192]{1,0:T(8,128)}), f32[32,8192]{1,0:T(8,128)}) %all-reduce.2.cloned.1.call-update) | async-done | bytes 1048592 | tf_op jit(solution)/shard_map/psum | solution.py:47
  223.0 2.1 multiply_reduce_fusion
  225.1 26.2 %psum.15 = f32[]{:T(128)} all-reduce(f32[]{:T(128)} %multiply_reduce_fusion), channel_id=1, replica_groups=mesh['rep'=16,'fsdp'=16] {'fsdp'}, use_global_device_ids=true, to_apply=%region_3.0 | all-reduce | flops 1 | bytes 8 | tf_op jit(solution)/shard_map/psum | solution.py:48
  252.0 0.0 copy-done.2
  252.0 2.8 %multiply_subtract_fusion = (f32[32,8192]{1,0:T(8,128)}, f32[32,8192]{1,0:T(8,128)}) fusion(f32[32,8192]{1,0:T(8,128)S(1)} %copy-done.1, f32[32,8192]{1,0:T(8,128)} %all-reduce.2.cloned.1.call-done, f32[]{:T(128)S(6)} %mul.75, f32[32,8192]{1,0:T(8,128)S(1)} %copy-done.2), kind=kLoop, calls=%fused_computation.10 | loop fusion | flops 1835008 | bytes 5242884 | tf_op jit(solution)/shard_map/sub | solution.py:20
Async XLA Ops:
  7.2 1.0 copy-start
  7.2 115.9 %reduce-scatter.2.cloned.1.call-start = ((), (), s32[]{:S(2)}) async-start(), calls=%async_computation.1 | async-start | bytes 17825792 | tf_op jit(solution)/shard_map/reduce_scatter | solution.py:28
  19.7 103.4 %copy-start.1 = (f32[32,8192]{1,0:T(8,128)S(1)}, f32[32,8192]{1,0:T(8,128)}, u32[]{:S(2)}) copy-start(f32[32,8192]{1,0:T(8,128)} %param.9) | copy-start | bytes 3145732
  19.7 232.3 %copy-start.2 = (f32[32,8192]{1,0:T(8,128)S(1)}, f32[32,8192]{1,0:T(8,128)}, u32[]{:S(2)}) copy-start(f32[32,8192]{1,0:T(8,128)} %param.13) | copy-start | bytes 3145732
  19.7 203.3 %all-reduce.2.cloned.1.call-start = ((), (), s32[]{:S(2)}) async-start(), calls=%async_computation.2 | async-start | bytes 2097152 | tf_op jit(solution)/shard_map/psum | solution.py:47
Sparse Core Ops, SparseCore 0:
  19.8 103.2 reduce-scatter.1
  127.6 95.3 all-reduce.1
where the time goes:
time: 262 us
  waiting for transfers between devices  199 us (76%)
  blocking collectives  26.2 us (10%)
  between operations  14.8 us (6%)
  matrix products  11.5 us (4%)
  other arithmetic  9.23 us (4%)
    reduce_scatter x1, waiting for transfers between devices, per_device(): lax.psum_scatter(lax.dot_general(activations, cotangent, (((0,), (0,)), (...  103 us
    psum x1, waiting for transfers between devices, per_device(): average = lax.psum(pseudo, 'rep') / replicas  95.5 us
    psum x1, blocking collectives, per_device(): squares = lax.psum(jnp.sum(average * average), 'fsdp')  26.2 us
    dot_general x1, matrix products, per_device(): lax.dot_general(activations, cotangent, (((0,), (0,)), ((), ())), preferr...  11.5 us
  transfers between devices with their start and end apart: 2, of which 2 were waited for; matrix products, arithmetic and copies ran while one was open for 0% of the time, Pallas kernels for 0%

commit v1 on v0

--- a/solution.py
+++ b/solution.py
@@ -1,3 +1,4 @@
+import functools
 import math
 import jax
 import jax.numpy as jnp
@@ -12,6 +13,14 @@
 decay_weight = 0.1
 outer_rate = 0.7
 momentum_coef = 0.9
+
+
+def map_scenes(message, named_axis):
+    kept_arr = jax.lax.all_gather(message, named_axis)
+    return jnp.sum(kept_arr, 0)
+
+
+group_put = functools.partial(map_scenes, named_axis="rep")
 
 
 def outer_update(average, squares, ceiling, momentum_old, anchor_old):
@@ -44,7 +53,7 @@
     pseudo = inner_rate * update - own_drift
     replicas = lax.axis_size("rep")
     ceiling = 0.3 * math.sqrt(rows_dev * lax.axis_size("fsdp") * D)
-    average = lax.psum(pseudo, "rep") / replicas
+    average = group_put(pseudo) / replicas
     squares = lax.psum(jnp.sum(average * average), "fsdp")
     momentum, updated = outer_update(average, squares, ceiling, outer_momentum, anchor)
     return (moment_one[None], moment_two[None], momentum, updated)

time: 262 us -> 288 us (1.099)
  waiting for transfers between devices: 199 us -> 219 us
  other arithmetic: 9.23 us -> 14.3 us
    all_gather x0 -> x1, waiting for transfers between devices: none -> 116 us  [map_scenes(): kept_arr = jax.lax.all_gather(message, named_axis)]
    psum x1 -> x0, waiting for transfers between devices: 95.5 us -> none  [per_device(): average = lax.psum(pseudo, 'rep') / replicas]
    reduce_sum x0 -> x1, other arithmetic: none -> 6.66 us  [map_scenes(): return jnp.sum(kept_arr, 0)]
where the time goes in v1:
time: 288 us; the launch traced here: 286 us
  waiting for transfers between devices  219 us (76%)
  blocking collectives  24.7 us (9%)
  between operations  14.8 us (5%)
  other arithmetic  14.3 us (5%)
  matrix products  11.5 us (4%)
    all_gather x1, waiting for transfers between devices, map_scenes(): kept_arr = jax.lax.all_gather(message, named_axis)  116 us
    reduce_scatter x1, waiting for transfers between devices, per_device(): lax.psum_scatter(lax.dot_general(activations, cotangent, (((0,), (0,)), (...  103 us
    psum x1, blocking collectives, per_device(): squares = lax.psum(jnp.sum(average * average), 'fsdp')  24.7 us
    dot_general x1, matrix products, per_device(): lax.dot_general(activations, cotangent, (((0,), (0,)), ((), ())), preferr...  11.5 us
    reduce_sum x1, other arithmetic, map_scenes(): return jnp.sum(kept_arr, 0)  6.66 us
  transfers between devices with their start and end apart: 2, of which 2 were waited for; matrix products, arithmetic and copies ran while one was open for 0% of the time, Pallas kernels for 0%

profile of v1, /device:TPU:1, one launch (start us, length us, event | category | flops | bytes accessed | tf_op | source)
XLA Modules:
  0.0 285.9 jit_solution(11861633441816778142)
XLA Ops:
  7.2 0.0 copy-start
  7.2 0.0 reduce-scatter.2.cloned.1.call-start
  7.2 1.0 copy-done
  8.2 11.5 %fusion = f32[512,8192]{1,0:T(8,128)} fusion(bf16[1,512,8192]{2,1,0:T(8,128)(2,1)} %param.8, bf16[1,512,512]{2,1,0:T(8,128)(2,1)S(1)} %copy-done), kind=kOutput, calls=%fused_computation | convolution fusion | flops 4294967296 | bytes 25690112 | tf_op jit(solution)/shard_map/dot_general | solution.py:38
  19.7 0.0 copy-start.1
  19.7 0.0 copy-start.2
  19.7 0.0 reduce-scatter.2.cloned.1.call-update
  19.7 0.0 all-gather.3.cloned.1.call-start
  19.8 103.3 %reduce-scatter.2.cloned.1.call-done = f32[32,8192]{1,0:T(8,128)} async-done(((f32[512,8192]{1,0:T(8,128)}), f32[32,8192]{1,0:T(8,128)}) %reduce-scatter.2.cloned.1.call-update) | async-done | bytes 1048592 | tf_op jit(solution)/shard_map/reduce_scatter | solution.py:37
  123.1 0.0 copy-done.1
  123.1 0.0 copy-done.2
  123.1 4.0 %bitcast_subtract_fusion = (f32[32,8192]{1,0:T(8,128)}, f32[1,32,8192]{2,1,0:T(8,128)}, f32[1,32,8192]{2,1,0:T(8,128)}) fusion(f32[1,32,8192]{2,1,0:T(8,128)S(1)} %copy-done.2, f32[32,8192]{1,0:T(8,128)S(1)} %copy-done.1, f32[32,8192]{1,0:T(8,128)} %reduce-scatter.2.cloned.1.call-done, f32[1,32,8192]{2,1,0:T(8,128)} %param.11, f32[1,32,8192]{2,1,0:T(8,128)} %param.12), kind=kLoop, calls=%fused_computation.4 | loop fusion | flops 4194304 | bytes 8388608 | tf_op jit(solution)/shard_map/sub | solution.py:53
  127.2 0.0 all-gather.3.cloned.1.call-update
  127.2 116.1 %all-gather.3.cloned.1.call-done = f32[512,8192]{1,0:T(8,128)} async-done(((f32[32,8192]{1,0:T(8,128)}), f32[512,8192]{1,0:T(8,128)}) %all-gather.3.cloned.1.call-update) | async-done | bytes 16777232 | tf_op jit(solution)/shard_map/all_gather | solution.py:19
  243.3 6.7 %reduce_sum.18 = f32[32,8192]{1,0:T(8,128)S(1)} reduce(f32[16,32,8192]{2,1,0:T(8,128)} %bitcast.34, f32[]{:T(128)} %constant.11.clone.1), dimensions={0}, to_apply=%region_1.0 | reduce | flops 3932160 | bytes 17825796 | tf_op jit(solution)/shard_map/reduce_sum | solution.py:20
  250.0 0.9 multiply_reduce_fusion
  250.8 24.7 %psum.7 = f32[]{:T(128)} all-reduce(f32[]{:T(128)} %multiply_reduce_fusion), channel_id=1, replica_groups=mesh['rep'=16,'fsdp'=16] {'fsdp'}, use_global_device_ids=true, to_apply=%region_3.0 | all-reduce | flops 1 | bytes 8 | tf_op jit(solution)/shard_map/psum | solution.py:57
  276.3 2.8 multiply_subtract_fusion
Async XLA Ops:
  7.2 1.0 copy-start
  7.2 115.9 %reduce-scatter.2.cloned.1.call-start = ((), (), s32[]{:S(2)}) async-start(), calls=%async_computation.1 | async-start | bytes 17825792 | tf_op jit(solution)/shard_map/reduce_scatter | solution.py:37
  19.7 103.4 %copy-start.1 = (f32[32,8192]{1,0:T(8,128)S(1)}, f32[32,8192]{1,0:T(8,128)}, u32[]{:S(2)}) copy-start(f32[32,8192]{1,0:T(8,128)} %param.9) | copy-start | bytes 3145732
  19.7 103.4 %copy-start.2 = (f32[1,32,8192]{2,1,0:T(8,128)S(1)}, f32[1,32,8192]{2,1,0:T(8,128)}, u32[]{:S(2)}) copy-start(f32[1,32,8192]{2,1,0:T(8,128)} %param.10) | copy-start | bytes 3145732
  19.7 223.6 %all-gather.3.cloned.1.call-start = ((), (), s32[]{:S(2)}) async-start(), calls=%async_computation.2 | async-start | bytes 17825792 | tf_op jit(solution)/shard_map/all_gather | solution.py:19
Sparse Core Ops, SparseCore 0:
  19.8 103.2 reduce-scatter.1
  127.3 115.9 all-gather.2
